TPU v7x, 32 devices: a whole 2x2x4 slice. The times are simulated.
32 devices in a mesh: mem: 8 (over z, y), job: 4 (over x, core).
Axes of the slice: x: 2, y: 2, z: 4, core: 2. Of those that a mesh axis runs over, the one named last changes fastest.
Arguments:
- pair_cost: bfloat16 [1536, 128, 128], P(('mem', 'job')), may hold values from -6 to 6
- pair_coef: bfloat16 [1536, 128, 128], P(('mem', 'job')), may hold values from 0.049804688 to 0.5
- slot_member: int32 [32, 48], P(('mem', 'job')), may hold values from 0 to 31, never falling along the last dimension, each value on 1 to 4 neighbouring positions
- slot_owner: int32 [32, 48, 1], P(('mem', 'job')), may hold values from 0 to 7; in each aligned block of 48 rows (0 to 47, 48 to 95, ..., all dimensions but the last counted through in order) at most 9 rows name the same one
- slot_local: int32 [32, 48], P(('mem', 'job')), may hold values from 0 to 15
- duals: float32 [512, 128], P(('mem', 'job')), may hold values from 0.1 to 3
- capacity: int32 [512, 128], P(('mem', 'job')), may hold values from 0 to 39
Outputs:
- primal: bfloat16 [1536, 128, 128], P(('mem', 'job'))
- gradient: float32 [512, 128], P(('mem', 'job'))
- member_share: float32 [256, 128], P('mem')
Inputs may be any that keep to these rules, and one draw needn't show every extreme that they name: `slot_member`: in each device's row the values never fall, every value appears, none more than 4 times, and one exactly 4 times. `slot_owner`: among the 48 entries of one device no value appears more than 9 times, and in some devices one appears exactly 9 times.
All inputs are finite; a program needn't handle non-finite values.
Results may differ from a plain program's by a relative error of at most 0.001.
Values sent between devices are 32-bit elements; how exact they have to be, the bound alone decides.
A program may use at most 64 MiB of HBM per device.

v0:
```python
import jax
import jax.numpy as jnp
from jax import lax
from jax.sharding import PartitionSpec as P

MB_DEV = 32
RIDGE = 1.0


def allocate(pair_cost, pair_coef, dual_rows):
    reduced = pair_cost.astype(jnp.float32) + pair_coef.astype(jnp.float32) * dual_rows[:, None, :]
    allocation = jnp.clip(-reduced / RIDGE, 0.0, 1.0)
    column_part = jnp.sum(pair_coef.astype(jnp.float32) * allocation, axis=1)
    row_part = jnp.sum(allocation, axis=2)
    return (allocation.astype(jnp.bfloat16), column_part, row_part)


def per_device(pair_cost, pair_coef, slot_member, slot_owner, slot_local, duals, capacity):
    slot_count = pair_cost.shape[0]
    block_size = pair_cost.shape[1]
    job_blocks = duals.shape[0]
    mem_count = lax.axis_size("mem")
    owner_index = slot_owner[0, :, 0]
    local_index = slot_local[0]
    peer_slots = max(2, (3 * slot_count + 2 * mem_count - 1) // (2 * mem_count))
    owner_table = (owner_index[:, None] == jnp.arange(mem_count, dtype=jnp.int32)[None, :]).astype(
        jnp.int32
    )
    slot_rank = jnp.sum((jnp.cumsum(owner_table, axis=0) - owner_table) * owner_table, axis=1)
    position = owner_index * peer_slots + slot_rank
    requests = jnp.zeros((mem_count * peer_slots,), jnp.int32).at[position].set(local_index)
    requests = requests.reshape(mem_count, peer_slots)
    received = lax.all_to_all(requests, "mem", split_axis=0, concat_axis=0, tiled=True)
    replies = duals[received]
    fetched, received = (
        lax.all_to_all(replies, "mem", split_axis=0, concat_axis=0, tiled=True),
        received,
    )
    dual_rows = fetched.reshape(mem_count * peer_slots, block_size)[position]
    primal, column_part, row_part = allocate(pair_cost, pair_coef, dual_rows)
    outgoing = (
        jnp.zeros((mem_count * peer_slots, block_size), jnp.float32).at[position].set(column_part)
    )
    incoming = lax.all_to_all(
        outgoing.reshape(mem_count, peer_slots, block_size),
        "mem",
        split_axis=0,
        concat_axis=0,
        tiled=True,
    )
    totals = jax.ops.segment_sum(
        incoming.reshape(mem_count * peer_slots, block_size),
        received.reshape(-1),
        num_segments=job_blocks,
    )
    gradient = totals - capacity.astype(jnp.float32)
    member_table = (jnp.arange(MB_DEV, dtype=jnp.int32)[:, None] == slot_member[0][None, :]).astype(
        jnp.float32
    )
    member_part = jnp.dot(
        member_table, row_part, precision=lax.Precision.HIGHEST, preferred_element_type=jnp.float32
    )
    member_share = lax.psum(member_part, "job") / block_size
    return (primal, gradient, member_share)


def solution(mesh):
    placed = (
        P(("mem", "job"), None, None),
        P(("mem", "job"), None, None),
        P(("mem", "job"), None),
        P(("mem", "job"), None, None),
        P(("mem", "job"), None),
        P(("mem", "job"), None),
        P(("mem", "job"), None),
    )
    return jax.shard_map(
        per_device,
        mesh=mesh,
        in_specs=placed,
        out_specs=(P(("mem", "job"), None, None), P(("mem", "job"), None), P("mem", None)),
        check_vma=False,
    )
```

profile of v0, /device:TPU:0, one launch (start us, length us, event | category | flops | bytes accessed | tf_op | source)
XLA Modules:
  0.0 57.0 jit_solution(11159333356886695551)
XLA Ops:
  0.6 0.0 copy-start
  0.6 0.7 %fusion.6 = s32[48,8]{1,0:T(8,128)S(1)} fusion(s32[48]{0:T(128)} %bitcast.20), kind=kLoop, calls=%fused_computation.15 | loop fusion | flops 768 | bytes 1728 | tf_op jit(solution)/shard_map/convert_element_type | solution.py:26
  1.4 0.1 reduce_window_sum.11
  1.5 0.8 %select_reduce_fusion = s32[48]{0:T(128)S(1)} fusion(s32[48,8]{1,0:T(8,128)S(1)} %reduce_window_sum.11, s32[48]{0:T(128)} %bitcast.21), kind=kLoop, calls=%fused_computation.13 | loop fusion | flops 1872 | bytes 1920 | tf_op jit(solution)/shard_map/reduce_sum | solution.py:29
  2.3 0.7 %fusion.13 = s32[48]{0:T(128)S(1)} fusion(s32[48]{0:T(128)S(1)} %select_reduce_fusion, s32[1,48,1]{1,2,0:T(1,128)} %param.10), kind=kLoop, calls=%fused_computation.29 | loop fusion | flops 240 | bytes 576 | tf_op jit(solution)/shard_map/select_n | solution.py:31
  3.0 0.9 %scatter_custom_fusion = s32[72]{0:T(128)S(1)} fusion(s32[48]{0:T(128)S(1)} %fusion.13, s32[48]{0:T(128)} %bitcast.23, s32[]{:T(128)} %constant.8.clone.1), kind=kCustom, calls=%fused_computation.31 | custom fusion | bytes 800 | tf_op jit(solution)/shard_map/scatter | solution.py:31
  3.8 0.1 all_to_all.14
  3.9 13.6 %all_to_all.22 = s32[8,1,9]{2,1,0:T(1,128)S(1)} all-to-all(s32[8,1,9]{2,1,0:T(1,128)S(1)} %bitcast.19), channel_id=1, replica_groups=mesh['mem'=8,'job'=4] {'mem'}, dimensions={0} | all-to-all | bytes 576 | tf_op jit(solution)/shard_map/all_to_all | solution.py:33
  17.5 0.1 reshape.83
  17.6 0.0 copy-done
  17.6 0.6 %gather_fusion = f32[72,128]{1,0:T(8,128)S(1)} fusion(f32[16,128]{1,0:T(8,128)S(1)} %copy-done, s32[1024]{0:T(1024)S(1)} %pad_clamp_fusion.1), kind=kCustom, calls=%fused_computation | custom fusion | bytes 74016 | tf_op jit(solution)/shard_map/gather | solution.py:34
  18.2 0.6 %reshape.82 = f32[8,9,128]{2,1,0:T(8,128)} reshape(f32[72,128]{1,0:T(8,128)S(1)} %gather_fusion) | data formatting | bytes 73728 | tf_op jit(solution)/shard_map/gather | solution.py:34
  18.8 3.4 %all-to-all-start.1 = ((f32[8,9,128]{2,1,0:T(8,128)}), f32[8,9,128]{2,1,0:T(8,128)S(1)}, u32[]{:S(2)}, u32[]{:S(2)}) async-start(f32[8,9,128]{2,1,0:T(8,128)} %reshape.82), calls=%async_computation.1 | async-start | bytes 131072 | tf_op jit(solution)/shard_map/all_to_all | solution.py:36
  22.2 0.5 broadcast.65
  22.7 0.7 %reduce.3 = s32[8,9]{1,0:T(8,128)S(1)} reduce(s32[8,1,9]{2,1,0:T(1,128)S(1)} %all_to_all.22, s32[]{:T(128)} %broadcast.65), dimensions={1}, to_apply=%all_to_all.15.reduce_sub_computation.3 | reduce | bytes 580 | tf_op jit(solution)/shard_map/all_to_all | solution.py:33
  23.4 0.1 reshape.115
  23.5 5.6 %all-to-all-done.1 = f32[8,9,128]{2,1,0:T(8,128)S(1)} async-done(((f32[8,9,128]{2,1,0:T(8,128)}), f32[8,9,128]{2,1,0:T(8,128)S(1)}, u32[]{:S(2)}, u32[]{:S(2)}) %all-to-all-start.1) | async-done | bytes 36896 | tf_op jit(solution)/shard_map/all_to_all | solution.py:36
  29.0 0.6 %gather_fusion.1 = f32[48,128]{1,0:T(8,128)S(1)} fusion(f32[72,128]{1,0:T(8,128)S(1)} %reshape.78, s32[1024]{0:T(1024)S(1)} %pad_clamp_fusion), kind=kCustom, calls=%fused_computation.1 | custom fusion | bytes 49344 | tf_op jit(solution)/shard_map/gather | solution.py:39
  29.6 0.0 copy-start.2
  29.6 0.0 copy-start.1
  29.6 4.1 %fusion.4 = (f32[48,128]{1,0:T(8,128)S(1)}, f32[48,128]{1,0:T(8,128)S(1)}, bf16[48,128,128]{2,1,0:T(8,128)(2,1)}) fusion(bf16[48,128,128]{2,1,0:T(8,128)(2,1)} %param.8, bf16[48,128,128]{2,1,0:T(8,128)(2,1)} %param.7, f32[48,128]{1,0:T(8,128)S(1)} %gather_fusion.1), kind=kLoop, calls=%fused_computation.11 | loop fusion | flops 7852032 | bytes 4792320 | tf_op jit(solution)/shard_map/reduce_sum | solution.py:14
  33.8 0.0 copy-done.2
  33.8 0.1 fusion.9
  33.9 10.1 %psum.7 = f32[32,128]{1,0:T(8,128)S(1)} all-reduce(f32[32,128]{1,0:T(8,128)S(1)} %fusion.9), channel_id=1, replica_groups=mesh['mem'=8,'job'=4] {'job'}, use_global_device_ids=true, to_apply=%region_7.8 | all-reduce | flops 4096 | bytes 32768 | tf_op jit(solution)/shard_map/psum | solution.py:63
  44.0 0.7 %scatter_custom_fusion.1 = f32[72,128]{1,0:T(8,128)S(1)} fusion(s32[48]{0:T(128)S(1)} %fusion.13, f32[48,128]{1,0:T(8,128)S(1)} %get-tuple-element.4, f32[]{:T(128)} %constant.7.clone.1), kind=kCustom, calls=%fused_computation.16 | custom fusion | bytes 36868 | tf_op jit(solution)/shard_map/scatter | solution.py:42
  44.7 0.6 %reshape.79 = f32[8,9,128]{2,1,0:T(8,128)} reshape(f32[72,128]{1,0:T(8,128)S(1)} %scatter_custom_fusion.1) | data formatting | bytes 73728 | tf_op jit(solution)/shard_map/reshape | solution.py:45
  45.3 3.3 %all-to-all-start.2 = ((f32[8,9,128]{2,1,0:T(8,128)}), f32[8,9,128]{2,1,0:T(8,128)S(1)}, u32[]{:S(2)}, u32[]{:S(2)}) async-start(f32[8,9,128]{2,1,0:T(8,128)} %reshape.79), calls=%async_computation.2 | async-start | bytes 131072 | tf_op jit(solution)/shard_map/all_to_all | solution.py:44
  48.7 0.6 %broadcast_multiply_fusion = f32[32,128]{1,0:T(8,128)} fusion(f32[32,128]{1,0:T(8,128)S(1)} %psum.7), kind=kLoop, calls=%fused_computation.21 | loop fusion | flops 4096 | bytes 32768 | tf_op jit(solution)/shard_map/div | solution.py:63
  49.3 6.2 %all-to-all-done.2 = f32[8,9,128]{2,1,0:T(8,128)S(1)} async-done(((f32[8,9,128]{2,1,0:T(8,128)}), f32[8,9,128]{2,1,0:T(8,128)S(1)}, u32[]{:S(2)}, u32[]{:S(2)}) %all-to-all-start.2) | async-done | bytes 36896 | tf_op jit(solution)/shard_map/all_to_all | solution.py:44
  55.5 0.8 %scatter_custom_fusion.2 = f32[16,128]{1,0:T(8,128)S(1)} fusion(s32[72]{0:T(128)S(1)} %reshape.115, f32[72,128]{1,0:T(8,128)S(1)} %reshape.117, f32[]{:T(128)} %constant.7.clone.1), kind=kCustom, calls=%fused_computation.26 | custom fusion | flops 9216 | bytes 8196 | tf_op jit(solution)/shard_map/scatter-add | solution.py:51
  56.3 0.0 copy-done.1
  56.3 0.6 %convert_subtract_fusion = f32[16,128]{1,0:T(8,128)} fusion(f32[16,128]{1,0:T(8,128)S(1)} %scatter_custom_fusion.2, s32[16,128]{1,0:T(8,128)S(1)} %copy-done.1), kind=kLoop, calls=%fused_computation.23 | loop fusion | flops 4096 | bytes 24576 | tf_op jit(solution)/shard_map/sub | solution.py:56
  (5 shorter events, 0.0 us)
Async XLA Ops:
  0.6 17.0 %copy-start = (f32[16,128]{1,0:T(8,128)S(1)}, f32[16,128]{1,0:T(8,128)}, u32[]{:S(2)}) copy-start(f32[16,128]{1,0:T(8,128)} %param.12) | copy-start | bytes 24580
  18.8 10.2 %all-to-all-start.1 = ((f32[8,9,128]{2,1,0:T(8,128)}), f32[8,9,128]{2,1,0:T(8,128)S(1)}, u32[]{:S(2)}, u32[]{:S(2)}) async-start(f32[8,9,128]{2,1,0:T(8,128)} %reshape.82), calls=%async_computation.1 | async-start | bytes 131072 | tf_op jit(solution)/shard_map/all_to_all | solution.py:36
  29.6 4.1 %copy-start.2 = (s32[1,48]{1,0:T(1,128)S(1)}, s32[1,48]{1,0:T(1,128)}, u32[]{:S(2)}) copy-start(s32[1,48]{1,0:T(1,128)} %param.9) | copy-start | bytes 580
  29.6 26.7 %copy-start.1 = (s32[16,128]{1,0:T(8,128)S(1)}, s32[16,128]{1,0:T(8,128)}, u32[]{:S(2)}) copy-start(s32[16,128]{1,0:T(8,128)} %param.13) | copy-start | bytes 24580
  45.3 10.2 %all-to-all-start.2 = ((f32[8,9,128]{2,1,0:T(8,128)}), f32[8,9,128]{2,1,0:T(8,128)S(1)}, u32[]{:S(2)}, u32[]{:S(2)}) async-start(f32[8,9,128]{2,1,0:T(8,128)} %reshape.79), calls=%async_computation.2 | async-start | bytes 131072 | tf_op jit(solution)/shard_map/all_to_all | solution.py:44
where the time goes:
time: 57.4 us; the launch traced here: 57 us
  blocking collectives  23.7 us (41%)
  waiting for transfers between devices  11.8 us (21%)
  other arithmetic  9.12 us (16%)
  starting transfers between devices  6.7 us (12%)
  local copies, waits for them, and re-layouts  4.76 us (8%)
  between operations  0.73 us (1%)
    all_to_all x1, blocking collectives, per_device(): lax.all_to_all(requests, 'mem', split_axis=0, concat_axis=0, tiled=True)  13.6 us
    psum x1, blocking collectives, per_device(): member_share = lax.psum(member_part, 'job') / block_size  10.1 us
    all_to_all x1, waiting for transfers between devices, per_device(): lax.all_to_all(outgoing.reshape(mem_count, peer_slots, block_size), 'mem'...  6.23 us
    all_to_all x1, waiting for transfers between devices, per_device(): lax.all_to_all(replies, 'mem', split_axis=0, concat_axis=0, tiled=True)  5.57 us
    reduce_sum x1, other arithmetic, allocate(): row_part = jnp.sum(allocation, axis=2)  4.11 us
    all_to_all x1, starting transfers between devices, per_device(): lax.all_to_all(replies, 'mem', split_axis=0, concat_axis=0, tiled=True)  3.35 us
    all_to_all x1, starting transfers between devices, per_device(): lax.all_to_all(outgoing.reshape(mem_count, peer_slots, block_size), 'mem'...  3.35 us
    gather x2, local copies, waits for them, and re-layouts, per_device(): replies = duals[received]  1.24 us
  transfers between devices with their start and end apart: 2, of which 2 were waited for; matrix products, arithmetic and copies ran while one was open for 3% of the time, Pallas kernels for 0%

commit v1 on v0

--- a/solution.py
+++ b/solution.py
@@ -30,7 +30,18 @@
     position = owner_index * peer_slots + slot_rank
     requests = jnp.zeros((mem_count * peer_slots,), jnp.int32).at[position].set(local_index)
     requests = requests.reshape(mem_count, peer_slots)
-    received = lax.all_to_all(requests, "mem", split_axis=0, concat_axis=0, tiled=True)
+    ways, here = (lax.axis_size("mem"), lax.axis_index("mem"))
+    width = requests.shape[0] // ways
+    lengths = list(requests.shape)
+    lengths[0] = width
+    height = lengths[0]
+    lengths[0] = height * ways
+    received = jnp.zeros(lengths, requests.dtype)
+    for mask in range(ways):
+        part = lax.dynamic_slice_in_dim(requests, (here ^ mask) * width, width, axis=0)
+        if mask:
+            part = lax.ppermute(part, "mem", [(d, d ^ mask) for d in range(ways)])
+        received = lax.dynamic_update_slice_in_dim(received, part, (here ^ mask) * height, axis=0)
     replies = duals[received]
     fetched, received = (
         lax.all_to_all(replies, "mem", split_axis=0, concat_axis=0, tiled=True),

time: 57.4 us -> 67.3 us (1.17)
  starting transfers between devices: 6.7 us -> 23.6 us
  blocking collectives: 23.7 us -> 10.1 us
  waiting for transfers between devices: 11.8 us -> 19.3 us
    ppermute x0 -> x7, starting transfers between devices: none -> 14.4 us  [per_device(): part = lax.ppermute(part, 'mem', [(d, d ^ mask) for d in range(ways)])]
    all_to_all x1 -> x0, blocking collectives: 13.6 us -> none  [per_device(): lax.all_to_all(requests, 'mem', split_axis=0, concat_axis=0, tiled=True)]
    ppermute x0 -> x7, waiting for transfers between devices: none -> 6.25 us  [per_device(): part = lax.ppermute(part, 'mem', [(d, d ^ mask) for d in range(ways)])]
    all_to_all x1, starting transfers between devices: 3.35 us -> 5.92 us  [per_device(): lax.all_to_all(replies, 'mem', split_axis=0, concat_axis=0, tiled=True)]
    all_to_all x1, waiting for transfers between devices: 5.57 us -> 6.82 us  [per_device(): lax.all_to_all(replies, 'mem', split_axis=0, concat_axis=0, tiled=True)]
  transfers between devices with their start and end apart: 2 -> 9, of which waited for: 2 -> 5; matrix products, arithmetic and copies ran while one was open for 3% -> 1% of each run, Pallas kernels for 0% -> 0%
where the time goes in v1:
time: 67.3 us; the launch traced here: 67 us
  starting transfers between devices  23.6 us (35%)
  waiting for transfers between devices  19.3 us (29%)
  blocking collectives  10.1 us (15%)
  other arithmetic  8.46 us (13%)
  local copies, waits for them, and re-layouts  4.52 us (7%)
  between operations  0.79 us (1%)
    ppermute x7, starting transfers between devices, per_device(): part = lax.ppermute(part, 'mem', [(d, d ^ mask) for d in range(ways)])  14.4 us
    psum x1, blocking collectives, per_device(): member_share = lax.psum(member_part, 'job') / block_size  10.1 us
    all_to_all x1, waiting for transfers between devices, per_device(): lax.all_to_all(replies, 'mem', split_axis=0, concat_axis=0, tiled=True)  6.82 us
    ppermute x7, waiting for transfers between devices, per_device(): part = lax.ppermute(part, 'mem', [(d, d ^ mask) for d in range(ways)])  6.25 us
    all_to_all x1, waiting for transfers between devices, per_device(): lax.all_to_all(outgoing.reshape(mem_count, peer_slots, block_size), 'mem'...  6.23 us
    all_to_all x1, starting transfers between devices, per_device(): lax.all_to_all(replies, 'mem', split_axis=0, concat_axis=0, tiled=True)  5.92 us
    reduce_sum x1, other arithmetic, allocate(): row_part = jnp.sum(allocation, axis=2)  4.11 us
    all_to_all x1, starting transfers between devices, per_device(): lax.all_to_all(outgoing.reshape(mem_count, peer_slots, block_size), 'mem'...  3.35 us
  transfers between devices with their start and end apart: 9, of which 5 were waited for; matrix products, arithmetic and copies ran while one was open for 1% of the time, Pallas kernels for 0%

profile of v1, /device:TPU:0, one launch (start us, length us, event | category | flops | bytes accessed | tf_op | source)
XLA Modules:
  0.0 67.0 jit_solution(12992384645191144618)
XLA Ops:
  0.6 0.0 copy-start
  0.7 0.7 %fusion.6 = s32[48,8]{1,0:T(8,128)S(1)} fusion(s32[48]{0:T(128)} %bitcast.14), kind=kLoop, calls=%fused_computation.15 | loop fusion | flops 768 | bytes 1728 | tf_op jit(solution)/shard_map/convert_element_type | solution.py:26
  1.4 0.1 reduce_window_sum.11
  1.5 0.8 %select_reduce_fusion = s32[48]{0:T(128)S(1)} fusion(s32[48,8]{1,0:T(8,128)S(1)} %reduce_window_sum.11, s32[48]{0:T(128)} %bitcast.15), kind=kLoop, calls=%fused_computation.13 | loop fusion | flops 1872 | bytes 1920 | tf_op jit(solution)/shard_map/reduce_sum | solution.py:29
  2.3 0.7 fusion.13
  3.0 0.9 %scatter_custom_fusion = s32[72]{0:T(128)S(1)} fusion(s32[48]{0:T(128)S(1)} %fusion.13, s32[48]{0:T(128)} %bitcast.17, s32[]{:T(128)} %constant.18.clone.1), kind=kCustom, calls=%fused_computation.39 | custom fusion | bytes 800 | tf_op jit(solution)/shard_map/scatter | solution.py:31
  3.8 0.1 reshape.48
  4.0 6.1 %collective-permute-start.6 = (s32[1,9]{1,0:T(1,128)S(1)}, s32[1,9]{1,0:T(1,128)S(1)}, u32[]{:S(2)}, u32[]{:S(2)}) collective-permute-start(s32[1,9]{1,0:T(1,128)S(1)} %get-tuple-element.6), channel_id=1, source_target_pairs={{0,28},{4,24},{8,20},{12,16},{16,12},{20,8},{24,4},{28,0},{1,29},{... | collective-permute-start | bytes 116 | tf_op jit(solution)/shard_map/ppermute | solution.py:43
  10.0 0.2 collective-permute-start.5
  10.3 0.7 %collective-permute-start.4 = (s32[1,9]{1,0:T(1,128)S(1)}, s32[1,9]{1,0:T(1,128)S(1)}, u32[]{:S(2)}, u32[]{:S(2)}) collective-permute-start(s32[1,9]{1,0:T(1,128)S(1)} %get-tuple-element.8), channel_id=1, source_target_pairs={{0,20},{4,16},{8,28},{12,24},{16,4},{20,0},{24,12},{28,8},{1,21},{... | collective-permute-start | bytes 116 | tf_op jit(solution)/shard_map/ppermute | solution.py:43
  11.0 2.0 %collective-permute-start.3 = (s32[1,9]{1,0:T(1,128)S(1)}, s32[1,9]{1,0:T(1,128)S(1)}, u32[]{:S(2)}, u32[]{:S(2)}) collective-permute-start(s32[1,9]{1,0:T(1,128)S(1)} %get-tuple-element.9), channel_id=1, source_target_pairs={{0,16},{4,20},{8,24},{12,28},{16,0},{20,4},{24,8},{28,12},{1,17},{... | collective-permute-start | bytes 116 | tf_op jit(solution)/shard_map/ppermute | solution.py:43
  13.1 1.6 %collective-permute-start = (s32[1,9]{1,0:T(1,128)S(1)}, s32[1,9]{1,0:T(1,128)S(1)}, u32[]{:S(2)}, u32[]{:S(2)}) collective-permute-start(s32[1,9]{1,0:T(1,128)S(1)} %get-tuple-element.12), channel_id=1, source_target_pairs={{0,4},{4,0},{8,12},{12,8},{16,20},{20,16},{24,28},{28,24},{1,5},{5... | collective-permute-start | bytes 116 | tf_op jit(solution)/shard_map/ppermute | solution.py:43
  14.7 1.9 %collective-permute-done = s32[1,9]{1,0:T(1,128)S(1)} collective-permute-done((s32[1,9]{1,0:T(1,128)S(1)}, s32[1,9]{1,0:T(1,128)S(1)}, u32[]{:S(2)}, u32[]{:S(2)}) %collective-permute-start) | collective-permute-done | bytes 68 | tf_op jit(solution)/shard_map/ppermute | solution.py:43
  16.6 1.4 %collective-permute-start.1 = (s32[1,9]{1,0:T(1,128)S(1)}, s32[1,9]{1,0:T(1,128)S(1)}, u32[]{:S(2)}, u32[]{:S(2)}) collective-permute-start(s32[1,9]{1,0:T(1,128)S(1)} %get-tuple-element.11), channel_id=1, source_target_pairs={{0,8},{4,12},{8,0},{12,4},{16,24},{20,28},{24,16},{28,20},{1,9},{5... | collective-permute-start | bytes 116 | tf_op jit(solution)/shard_map/ppermute | solution.py:43
  18.0 2.2 %collective-permute-done.1 = s32[1,9]{1,0:T(1,128)S(1)} collective-permute-done((s32[1,9]{1,0:T(1,128)S(1)}, s32[1,9]{1,0:T(1,128)S(1)}, u32[]{:S(2)}, u32[]{:S(2)}) %collective-permute-start.1) | collective-permute-done | bytes 68 | tf_op jit(solution)/shard_map/ppermute | solution.py:43
  20.2 2.3 %collective-permute-start.2 = (s32[1,9]{1,0:T(1,128)S(1)}, s32[1,9]{1,0:T(1,128)S(1)}, u32[]{:S(2)}, u32[]{:S(2)}) collective-permute-start(s32[1,9]{1,0:T(1,128)S(1)} %get-tuple-element.10), channel_id=1, source_target_pairs={{0,12},{4,8},{8,4},{12,0},{16,28},{20,24},{24,20},{28,16},{1,13},{... | collective-permute-start | bytes 116 | tf_op jit(solution)/shard_map/ppermute | solution.py:43
  22.5 2.2 %collective-permute-done.2 = s32[1,9]{1,0:T(1,128)S(1)} collective-permute-done((s32[1,9]{1,0:T(1,128)S(1)}, s32[1,9]{1,0:T(1,128)S(1)}, u32[]{:S(2)}, u32[]{:S(2)}) %collective-permute-start.2) | collective-permute-done | bytes 68 | tf_op jit(solution)/shard_map/ppermute | solution.py:43
  24.7 0.0 collective-permute-done.3
  24.7 0.0 collective-permute-done.4
  24.8 0.0 collective-permute-done.5
  24.8 0.0 collective-permute-done.6
  24.9 0.1 reshape.54
  25.0 0.0 copy-done
  25.0 0.6 gather_fusion
  25.6 0.6 reshape.53
  26.2 5.9 %all-to-all-start = ((f32[8,9,128]{2,1,0:T(8,128)}), f32[8,9,128]{2,1,0:T(8,128)S(1)}, u32[]{:S(2)}, u32[]{:S(2)}) async-start(f32[8,9,128]{2,1,0:T(8,128)} %reshape.53), calls=%async_computation | async-start | bytes 131072 | tf_op jit(solution)/shard_map/all_to_all | solution.py:47
  32.1 0.1 reshape.86
  32.2 6.8 %all-to-all-done = f32[8,9,128]{2,1,0:T(8,128)S(1)} async-done(((f32[8,9,128]{2,1,0:T(8,128)}), f32[8,9,128]{2,1,0:T(8,128)S(1)}, u32[]{:S(2)}, u32[]{:S(2)}) %all-to-all-start) | async-done | bytes 36896 | tf_op jit(solution)/shard_map/all_to_all | solution.py:47
  39.0 0.6 gather_fusion.1
  39.6 0.0 copy-start.2
  39.6 0.0 copy-start.1
  39.6 4.1 %fusion.4 = (f32[48,128]{1,0:T(8,128)S(1)}, f32[48,128]{1,0:T(8,128)S(1)}, bf16[48,128,128]{2,1,0:T(8,128)(2,1)}) fusion(bf16[48,128,128]{2,1,0:T(8,128)(2,1)} %param.8, bf16[48,128,128]{2,1,0:T(8,128)(2,1)} %param.7, f32[48,128]{1,0:T(8,128)S(1)} %gather_fusion.1), kind=kLoop, calls=%fused_computation.11 | loop fusion | flops 7852032 | bytes 4792320 | tf_op jit(solution)/shard_map/reduce_sum | solution.py:14
  43.8 0.0 copy-done.2
  43.8 0.1 fusion.9
  43.9 10.1 %psum.7 = f32[32,128]{1,0:T(8,128)S(1)} all-reduce(f32[32,128]{1,0:T(8,128)S(1)} %fusion.9), channel_id=1, replica_groups=mesh['mem'=8,'job'=4] {'job'}, use_global_device_ids=true, to_apply=%region_7.8 | all-reduce | flops 4096 | bytes 32768 | tf_op jit(solution)/shard_map/psum | solution.py:74
  54.0 0.7 %scatter_custom_fusion.1 = f32[72,128]{1,0:T(8,128)S(1)} fusion(s32[48]{0:T(128)S(1)} %fusion.13, f32[48,128]{1,0:T(8,128)S(1)} %get-tuple-element.4, f32[]{:T(128)} %constant.17.clone.1), kind=kCustom, calls=%fused_computation.16 | custom fusion | bytes 36868 | tf_op jit(solution)/shard_map/scatter | solution.py:53
  54.7 0.6 reshape.50
  55.3 3.3 %all-to-all-start.1 = ((f32[8,9,128]{2,1,0:T(8,128)}), f32[8,9,128]{2,1,0:T(8,128)S(1)}, u32[]{:S(2)}, u32[]{:S(2)}) async-start(f32[8,9,128]{2,1,0:T(8,128)} %reshape.50), calls=%async_computation.1 | async-start | bytes 131072 | tf_op jit(solution)/shard_map/all_to_all | solution.py:55
  58.7 0.6 broadcast_multiply_fusion
  59.3 6.2 %all-to-all-done.1 = f32[8,9,128]{2,1,0:T(8,128)S(1)} async-done(((f32[8,9,128]{2,1,0:T(8,128)}), f32[8,9,128]{2,1,0:T(8,128)S(1)}, u32[]{:S(2)}, u32[]{:S(2)}) %all-to-all-start.1) | async-done | bytes 36896 | tf_op jit(solution)/shard_map/all_to_all | solution.py:55
  65.5 0.8 %scatter_custom_fusion.2 = f32[16,128]{1,0:T(8,128)S(1)} fusion(s32[72]{0:T(128)S(1)} %reshape.86, f32[72,128]{1,0:T(8,128)S(1)} %reshape.88, f32[]{:T(128)} %constant.17.clone.1), kind=kCustom, calls=%fused_computation.26 | custom fusion | flops 9216 | bytes 8196 | tf_op jit(solution)/shard_map/scatter-add | solution.py:62
  66.3 0.0 copy-done.1
  66.4 0.6 convert_subtract_fusion
  (15 shorter events, 0.3 us)
Async XLA Ops:
  0.6 24.3 %copy-start = (f32[16,128]{1,0:T(8,128)S(1)}, f32[16,128]{1,0:T(8,128)}, u32[]{:S(2)}) copy-start(f32[16,128]{1,0:T(8,128)} %param.12) | copy-start | bytes 24580
  4.0 20.9 %collective-permute-start.6 = (s32[1,9]{1,0:T(1,128)S(1)}, s32[1,9]{1,0:T(1,128)S(1)}, u32[]{:S(2)}, u32[]{:S(2)}) collective-permute-start(s32[1,9]{1,0:T(1,128)S(1)} %get-tuple-element.6), channel_id=1, source_target_pairs={{0,28},{4,24},{8,20},{12,16},{16,12},{20,8},{24,4},{28,0},{1,29},{... | collective-permute-start | bytes 116 | tf_op jit(solution)/shard_map/ppermute | solution.py:43
  10.0 14.7 %collective-permute-start.5 = (s32[1,9]{1,0:T(1,128)S(1)}, s32[1,9]{1,0:T(1,128)S(1)}, u32[]{:S(2)}, u32[]{:S(2)}) collective-permute-start(s32[1,9]{1,0:T(1,128)S(1)} %get-tuple-element.7), channel_id=1, source_target_pairs={{0,24},{4,28},{8,16},{12,20},{16,8},{20,12},{24,0},{28,4},{1,25},{... | collective-permute-start | bytes 116 | tf_op jit(solution)/shard_map/ppermute | solution.py:43
  10.3 14.5 %collective-permute-start.4 = (s32[1,9]{1,0:T(1,128)S(1)}, s32[1,9]{1,0:T(1,128)S(1)}, u32[]{:S(2)}, u32[]{:S(2)}) collective-permute-start(s32[1,9]{1,0:T(1,128)S(1)} %get-tuple-element.8), channel_id=1, source_target_pairs={{0,20},{4,16},{8,28},{12,24},{16,4},{20,0},{24,12},{28,8},{1,21},{... | collective-permute-start | bytes 116 | tf_op jit(solution)/shard_map/ppermute | solution.py:43
  11.0 13.7 %collective-permute-start.3 = (s32[1,9]{1,0:T(1,128)S(1)}, s32[1,9]{1,0:T(1,128)S(1)}, u32[]{:S(2)}, u32[]{:S(2)}) collective-permute-start(s32[1,9]{1,0:T(1,128)S(1)} %get-tuple-element.9), channel_id=1, source_target_pairs={{0,16},{4,20},{8,24},{12,28},{16,0},{20,4},{24,8},{28,12},{1,17},{... | collective-permute-start | bytes 116 | tf_op jit(solution)/shard_map/ppermute | solution.py:43
  13.1 3.6 %collective-permute-start = (s32[1,9]{1,0:T(1,128)S(1)}, s32[1,9]{1,0:T(1,128)S(1)}, u32[]{:S(2)}, u32[]{:S(2)}) collective-permute-start(s32[1,9]{1,0:T(1,128)S(1)} %get-tuple-element.12), channel_id=1, source_target_pairs={{0,4},{4,0},{8,12},{12,8},{16,20},{20,16},{24,28},{28,24},{1,5},{5... | collective-permute-start | bytes 116 | tf_op jit(solution)/shard_map/ppermute | solution.py:43
  16.6 3.6 %collective-permute-start.1 = (s32[1,9]{1,0:T(1,128)S(1)}, s32[1,9]{1,0:T(1,128)S(1)}, u32[]{:S(2)}, u32[]{:S(2)}) collective-permute-start(s32[1,9]{1,0:T(1,128)S(1)} %get-tuple-element.11), channel_id=1, source_target_pairs={{0,8},{4,12},{8,0},{12,4},{16,24},{20,28},{24,16},{28,20},{1,9},{5... | collective-permute-start | bytes 116 | tf_op jit(solution)/shard_map/ppermute | solution.py:43
  20.2 4.5 %collective-permute-start.2 = (s32[1,9]{1,0:T(1,128)S(1)}, s32[1,9]{1,0:T(1,128)S(1)}, u32[]{:S(2)}, u32[]{:S(2)}) collective-permute-start(s32[1,9]{1,0:T(1,128)S(1)} %get-tuple-element.10), channel_id=1, source_target_pairs={{0,12},{4,8},{8,4},{12,0},{16,28},{20,24},{24,20},{28,16},{1,13},{... | collective-permute-start | bytes 116 | tf_op jit(solution)/shard_map/ppermute | solution.py:43
  26.2 12.8 %all-to-all-start = ((f32[8,9,128]{2,1,0:T(8,128)}), f32[8,9,128]{2,1,0:T(8,128)S(1)}, u32[]{:S(2)}, u32[]{:S(2)}) async-start(f32[8,9,128]{2,1,0:T(8,128)} %reshape.53), calls=%async_computation | async-start | bytes 131072 | tf_op jit(solution)/shard_map/all_to_all | solution.py:47
  39.6 4.1 %copy-start.2 = (s32[1,48]{1,0:T(1,128)S(1)}, s32[1,48]{1,0:T(1,128)}, u32[]{:S(2)}) copy-start(s32[1,48]{1,0:T(1,128)} %param.9) | copy-start | bytes 580
  39.6 26.7 %copy-start.1 = (s32[16,128]{1,0:T(8,128)S(1)}, s32[16,128]{1,0:T(8,128)}, u32[]{:S(2)}) copy-start(s32[16,128]{1,0:T(8,128)} %param.13) | copy-start | bytes 24580
  55.3 10.2 %all-to-all-start.1 = ((f32[8,9,128]{2,1,0:T(8,128)}), f32[8,9,128]{2,1,0:T(8,128)S(1)}, u32[]{:S(2)}, u32[]{:S(2)}) async-start(f32[8,9,128]{2,1,0:T(8,128)} %reshape.50), calls=%async_computation.1 | async-start | bytes 131072 | tf_op jit(solution)/shard_map/all_to_all | solution.py:55
